TPU v7x, 32 devices: a whole 2x2x4 slice. The times are simulated.
32 devices in a mesh: wide: 8 (over y, x, core), by: 4 (over z).
Axes of the slice: x: 2, y: 2, z: 4, core: 2. Of those that a mesh axis runs over, the one named last changes fastest.
Arguments:
- tiles: float32 [704, 512, 512], P(('wide', 'by')), may hold values from -6 to 6
- tile_rows: int32 [704], P(('wide', 'by')), may hold values from 0 to 7
- tile_cols: int32 [704], P(('wide', 'by')), may hold values from 0 to 63, as said below
- start_panel: float32 [32768, 64], P('wide'), may hold values from -6 to 6
Outputs:
- panel: float32 [32768, 64], P('wide')
- factor: float32 [64, 64], replicated
Inputs may be any that keep to these rules, and one draw needn't show every extreme that they name: `tile_cols`: within one device's 22 tiles, at most 3 have block columns in the block rows of one index of wide, and one index of wide takes exactly 3 of them.
All inputs are finite; a program needn't handle non-finite values.
Results may differ from a plain program's by a relative error of at most 0.0001.
Values sent between devices are 32-bit elements; how exact they have to be, the bound alone decides.
No kernel may reach another device: no remote copies, remote signals or barrier semaphores. Data moves between devices by JAX's collectives and lax.ppermute only.
A program may use at most 192 MiB of HBM per device.

v0:
```python
import jax
import jax.numpy as jnp
from jax import lax
from jax.sharding import PartitionSpec as P

ITERS = 2


def local(tiles, tile_rows, tile_cols, start_panel):
    wide_count = lax.axis_size("wide")
    my_wide = lax.axis_index("wide")
    tile_count = tiles.shape[0]
    block_size = tiles.shape[1]
    width = start_panel.shape[1]
    block_rows = start_panel.shape[0] // block_size
    capacity = max(2, tile_count // wide_count + 1)
    slot_count = wide_count * capacity
    highest = lax.Precision.HIGHEST
    peer_index = tile_cols // block_rows
    positions = jnp.arange(tile_count, dtype=jnp.int32)
    earlier = positions[:, None] > positions[None, :]
    same_peer = peer_index[:, None] == peer_index[None, :]
    rank_within = jnp.sum((earlier & same_peer).astype(jnp.int32), axis=1)
    slot_of = peer_index * capacity + rank_within
    slot_match = slot_of[:, None] == jnp.arange(slot_count, dtype=jnp.int32)[None, :]
    slot_table = slot_match.astype(jnp.float32)
    request = jnp.sum(jnp.where(slot_match, tile_cols[:, None] + 1, 0), axis=0) - 1
    incoming = lax.all_to_all(
        request.reshape(wide_count, capacity), "wide", split_axis=0, concat_axis=0, tiled=True
    ).reshape(slot_count)
    local_in = incoming - my_wide * block_rows
    block_iota = jnp.arange(block_rows, dtype=jnp.int32)
    serve_table = (local_in[:, None] == block_iota[None, :]).astype(jnp.float32)
    row_table = (tile_rows[:, None] == block_iota[None, :]).astype(jnp.float32)
    panel = start_panel
    factor = jnp.zeros((width, width), jnp.float32)
    for step in range(ITERS):
        flat_panel = panel.reshape(block_rows, block_size * width)
        outgoing = jnp.dot(serve_table, flat_panel, precision=highest)
        received = lax.all_to_all(outgoing, "wide", split_axis=0, concat_axis=0, tiled=True)
        col_panels = jnp.dot(slot_table, received, precision=highest).reshape(
            tile_count, block_size, width
        )
        row_panels = jnp.dot(row_table, flat_panel, precision=highest).reshape(
            tile_count, block_size, width
        )
        direct = jnp.einsum("tab,tbk->tak", tiles, col_panels, precision=highest)
        mirror = jnp.einsum("tba,tbk->tak", tiles, row_panels, precision=highest)
        partial_rows = jnp.dot(
            row_table.T, direct.reshape(tile_count, block_size * width), precision=highest
        )
        mirror_flat = mirror.reshape(tile_count, block_size * width)
        placed = jnp.dot(slot_table.T, mirror_flat, precision=highest)
        returned = lax.all_to_all(placed, "wide", split_axis=0, concat_axis=0, tiled=True)
        partial_rows = partial_rows + jnp.dot(serve_table.T, returned, precision=highest)
        partial_rows = partial_rows.reshape(block_rows * block_size, width)
        image = lax.psum(partial_rows, "by")
        gram = lax.psum(jnp.dot(image.T, image, precision=highest), "wide")
        factor = jnp.linalg.cholesky(gram)
        panel = jax.scipy.linalg.solve_triangular(factor, image.T, lower=True).T
    return (panel, factor)


def solution(mesh):
    placed = (P(("wide", "by"), None, None), P(("wide", "by")), P(("wide", "by")), P("wide", None))
    return jax.shard_map(
        local, mesh=mesh, in_specs=placed, out_specs=(P("wide", None), P()), check_vma=False
    )
```

profile of v0, /device:TPU:0, one launch (start us, length us, event | category | flops | bytes accessed | tf_op | source)
XLA Modules:
  0.0 638.6 jit_solution(3037137050593948503)
XLA Ops:
  8.8 5.2 all-to-all-start
  22.6 21.3 %fusion.13 = f32[22,512,64]{1,2,0:T(8,128)} fusion(f32[22,512,512]{2,1,0:T(8,128)} %param.7, f32[22,512,64]{1,0,2:T(8,128)S(1)} %fusion.60), kind=kOutput, calls=%fused_computation.15 | convolution fusion | flops 4429185024 | bytes 28835840 | tf_op jit(solution)/shard_map/tba,tbk->tak/dot_general | solution.py:48
  43.9 5.3 copy.59
  49.2 6.3 reshape.153
  63.2 4.5 all-to-all-start.2
  75.3 41.6 %all-to-all-done.2 = f32[8,3,32768]{2,1,0:T(4,128)} async-done(((f32[8,3,32768]{2,1,0:T(4,128)}), f32[8,3,32768]{2,1,0:T(4,128)}, u32[]{:S(2)}, u32[]{:S(2)}) %all-to-all-start.2) | async-done | bytes 3145760 | tf_op jit(solution)/shard_map/all_to_all | solution.py:54
  116.9 4.5 all-to-all-start.1
  125.3 45.2 %all-to-all-done.1 = f32[8,3,32768]{2,1,0:T(4,128)} async-done(((f32[8,3,32768]{2,1,0:T(4,128)}), f32[8,3,32768]{2,1,0:T(4,128)}, u32[]{:S(2)}, u32[]{:S(2)}) %all-to-all-start.1) | async-done | bytes 3145760 | tf_op jit(solution)/shard_map/all_to_all | solution.py:40
  170.5 5.5 all_to_all.30
  176.0 6.4 %dot_general.80 = f32[512,64,24]{1,0,2:T(8,128)} reshape(f32[32768,24]{0,1:T(8,128)} %bitcast.82) | data formatting | bytes 6291456 | tf_op jit(solution)/shard_map/dot_general | solution.py:41
  182.4 6.6 %copy.54 = f32[512,64,24]{0,2,1:T(8,128)} copy(f32[512,64,24]{1,0,2:T(8,128)} %dot_general.80) | data formatting | bytes 6291456 | tf_op jit(solution)/shard_map/dot_general | solution.py:41
  192.6 27.3 %fusion.10 = f32[22,512,64]{1,2,0:T(8,128)} fusion(f32[22,512,512]{2,1,0:T(8,128)} %param.7, f32[22,512,64]{1,0,2:T(8,128)S(1)} %fusion.37), kind=kOutput, calls=%fused_computation.14 | convolution fusion | flops 4429185024 | bytes 28835840 | tf_op jit(solution)/shard_map/tab,tbk->tak/dot_general | solution.py:47
  219.9 5.3 copy.56
  225.3 6.5 %reshape.143 = f32[22,32768]{1,0:T(8,128)} reshape(f32[22,512,64]{2,1,0:T(8,128)} %copy.56) | data formatting | bytes 5767168 | tf_op jit(solution)/shard_map/reshape | solution.py:50
  240.5 86.1 %all-reduce.3.cloned.1.call-done = f32[4096,64]{1,0:T(8,128)} async-done(((f32[4096,64]{1,0:T(8,128)}), f32[4096,64]{1,0:T(8,128)}) %all-reduce.3.cloned.1.call-update) | async-done | bytes 1048592 | tf_op jit(solution)/shard_map/psum | solution.py:57
  326.6 5.9 fusion.68
  332.5 24.3 %psum.29 = f32[64,64]{0,1:T(8,128)S(1)} all-reduce(f32[64,64]{0,1:T(8,128)S(1)} %fusion.68), channel_id=1, replica_groups=mesh['wide'=8,'by'=4] {'wide'}, use_global_device_ids=true, to_apply=%region_3.4 | all-reduce | flops 4096 | bytes 32768 | tf_op jit(solution)/shard_map/psum | solution.py:58
  356.9 5.8 cholesky.44
  364.1 4.9 custom-call.6
  378.2 4.8 all-to-all-start.3
  386.9 19.4 %fusion.19 = f32[22,512,64]{1,2,0:T(8,128)S(1)} fusion(f32[22,512,512]{2,1,0:T(8,128)} %param.7, f32[22,512,64]{1,0,2:T(8,128)S(1)} %fusion.58), kind=kOutput, calls=%fused_computation.17 | convolution fusion | flops 4429185024 | bytes 28835840 | tf_op jit(solution)/shard_map/tba,tbk->tak/dot_general | solution.py:48
  410.2 4.6 reshape.155
  420.5 11.6 %all-to-all-done.3 = f32[8,3,32768]{2,1,0:T(4,128)} async-done(((f32[8,3,32768]{2,1,0:T(4,128)}), f32[8,3,32768]{2,1,0:T(4,128)}, u32[]{:S(2)}, u32[]{:S(2)}) %all-to-all-start.3) | async-done | bytes 3145760 | tf_op jit(solution)/shard_map/all_to_all | solution.py:40
  432.2 4.5 all-to-all-start.4
  440.5 4.9 dot_general.95
  445.4 5.0 copy.65
  452.1 25.6 %fusion.16 = f32[22,512,64]{1,2,0:T(8,128)S(1)} fusion(f32[22,512,512]{2,1,0:T(8,128)} %param.7, f32[22,512,64]{1,0,2:T(8,128)S(1)} %fusion.35), kind=kOutput, calls=%fused_computation.16 | convolution fusion | flops 4429185024 | bytes 28835840 | tf_op jit(solution)/shard_map/tab,tbk->tak/dot_general | solution.py:47
  498.9 86.2 %all-reduce.5.cloned.1.call-done = f32[4096,64]{1,0:T(8,128)} async-done(((f32[4096,64]{1,0:T(8,128)}), f32[4096,64]{1,0:T(8,128)}) %all-reduce.5.cloned.1.call-update) | async-done | bytes 1048592 | tf_op jit(solution)/shard_map/psum | solution.py:57
  585.1 5.9 fusion.69
  591.0 24.4 %psum.31 = f32[64,64]{0,1:T(8,128)S(1)} all-reduce(f32[64,64]{0,1:T(8,128)S(1)} %fusion.69), channel_id=1, replica_groups=mesh['wide'=8,'by'=4] {'wide'}, use_global_device_ids=true, to_apply=%region_7.10 | all-reduce | flops 4096 | bytes 32768 | tf_op jit(solution)/shard_map/psum | solution.py:58
  615.5 5.8 cholesky.55
  623.3 4.9 custom-call.7
  (69 shorter events, 97.6 us)
Async XLA Ops:
  8.8 54.4 %all-to-all-start = ((s32[8,1,3]{2,1,0:T(1,128)}), s32[8,1,3]{2,1,0:T(1,128)S(1)}, u32[]{:S(2)}, u32[]{:S(2)}) async-start(s32[8,1,3]{2,1,0:T(1,128)} %bitcast.1), calls=%async_computation | async-start | bytes 8192 | tf_op jit(solution)/shard_map/all_to_all | solution.py:28
  16.5 4.7 copy-start.2
  63.2 53.7 %all-to-all-start.2 = ((f32[8,3,32768]{2,1,0:T(4,128)}), f32[8,3,32768]{2,1,0:T(4,128)}, u32[]{:S(2)}, u32[]{:S(2)}) async-start(f32[8,3,32768]{2,1,0:T(4,128)} %copy.60), calls=%async_computation.2 | async-start | bytes 8388608 | tf_op jit(solution)/shard_map/all_to_all | solution.py:54
  116.9 53.7 %all-to-all-start.1 = ((f32[8,3,32768]{2,1,0:T(4,128)}), f32[8,3,32768]{2,1,0:T(4,128)}, u32[]{:S(2)}, u32[]{:S(2)}) async-start(f32[8,3,32768]{2,1,0:T(4,128)} %copy.53), calls=%async_computation.1 | async-start | bytes 8388608 | tf_op jit(solution)/shard_map/all_to_all | solution.py:40
  121.4 205.1 %all-reduce.3.cloned.1.call-start = ((), (), s32[]{:S(2)}) async-start(), calls=%async_computation.5 | async-start | bytes 4194304 | tf_op jit(solution)/shard_map/psum | solution.py:57
  326.6 42.5 %copy-start.1 = (f32[4096,64]{1,0:T(8,128)S(1)}, f32[4096,64]{1,0:T(8,128)}, u32[]{:S(2)}) copy-start(f32[4096,64]{1,0:T(8,128)} %all-reduce.3.cloned.1.call-done) | copy-start | bytes 3145732
  378.2 54.0 %all-to-all-start.3 = ((f32[8,3,32768]{2,1,0:T(4,128)}), f32[8,3,32768]{2,1,0:T(4,128)}, u32[]{:S(2)}, u32[]{:S(2)}) async-start(f32[8,3,32768]{2,1,0:T(4,128)} %copy.64), calls=%async_computation.3 | async-start | bytes 8388608 | tf_op jit(solution)/shard_map/all_to_all | solution.py:40
  432.2 56.1 %all-to-all-start.4 = ((f32[8,3,32768]{2,1,0:T(4,128)}), f32[8,3,32768]{2,1,0:T(4,128)}, u32[]{:S(2)}, u32[]{:S(2)}) async-start(f32[8,3,32768]{2,1,0:T(4,128)} %copy.71), calls=%async_computation.4 | async-start | bytes 8388608 | tf_op jit(solution)/shard_map/all_to_all | solution.py:54
  436.7 148.4 %all-reduce.5.cloned.1.call-start = ((), (), s32[]{:S(2)}) async-start(), calls=%async_computation.6 | async-start | bytes 4194304 | tf_op jit(solution)/shard_map/psum | solution.py:57
  585.1 43.1 %copy-start = (f32[4096,64]{1,0:T(8,128)S(1)}, f32[4096,64]{1,0:T(8,128)}, u32[]{:S(2)}) copy-start(f32[4096,64]{1,0:T(8,128)} %all-reduce.5.cloned.1.call-done) | copy-start | bytes 3145732
Sparse Core Ops, SparseCore 0:
  240.6 85.9 all-reduce.2
  499.0 86.0 all-reduce.4
where the time goes:
time: 648 us; the launch traced here: 639 us
  waiting for transfers between devices  271 us (42%)
  matrix products  138 us (21%)
  local copies, waits for them, and re-layouts  116 us (18%)
  blocking collectives  48.7 us (8%)
  other arithmetic  26.4 us (4%)
  starting transfers between devices  23.7 us (4%)
  between operations  14.6 us (2%)
    psum x2, waiting for transfers between devices, local(): image = lax.psum(partial_rows, 'by')  172 us
    all_to_all x2, waiting for transfers between devices, local(): lax.all_to_all(outgoing, 'wide', split_axis=0, concat_axis=0, tiled=True)  56.9 us
    dot_general x2, matrix products, local(): direct = jnp.einsum('tab,tbk->tak', tiles, col_panels, precision=highest)  52.9 us
    psum x2, blocking collectives, local(): gram = lax.psum(jnp.dot(image.T, image, precision=highest), 'wide')  48.7 us
    all_to_all x2, waiting for transfers between devices, local(): lax.all_to_all(placed, 'wide', split_axis=0, concat_axis=0, tiled=True)  41.6 us
    dot_general x2, matrix products, local(): mirror = jnp.einsum('tba,tbk->tak', tiles, row_panels, precision=highest)  40.7 us
    dot_general x4, local copies, waits for them, and re-layouts, local(): jnp.dot(slot_table, received, precision=highest)  22.9 us
    another operation x6, other arithmetic, local(): factor = jnp.linalg.cholesky(gram)  13 us
  transfers between devices with their start and end apart: 7, of which 5 were waited for; matrix products, arithmetic and copies ran while one was open for 22% of the time, Pallas kernels for 0%

commit v1 on v0

--- a/solution.py
+++ b/solution.py
@@ -4,6 +4,10 @@
 from jax.sharding import PartitionSpec as P
 
 ITERS = 2
+
+
+def wrap_the_pages(original, chip_axis):
+    return lax.all_gather(original, axis_name=chip_axis).sum(axis=0)
 
 
 def local(tiles, tile_rows, tile_cols, start_panel):
@@ -55,7 +59,7 @@
         partial_rows = partial_rows + jnp.dot(serve_table.T, returned, precision=highest)
         partial_rows = partial_rows.reshape(block_rows * block_size, width)
         image = lax.psum(partial_rows, "by")
-        gram = lax.psum(jnp.dot(image.T, image, precision=highest), "wide")
+        gram = wrap_the_pages(jnp.dot(image.T, image, precision=highest), chip_axis="wide")
         factor = jnp.linalg.cholesky(gram)
         panel = jax.scipy.linalg.solve_triangular(factor, image.T, lower=True).T
     return (panel, factor)

time: 648 us -> 618 us (0.954)
  blocking collectives: 48.7 us -> 18.9 us
    psum x2 -> x0, blocking collectives: 48.7 us -> none  [local(): gram = lax.psum(jnp.dot(image.T, image, precision=highest), 'wide')]
    all_gather x0 -> x2, blocking collectives: none -> 18.9 us  [wrap_the_pages(): return lax.all_gather(original, axis_name=chip_axis).sum(axis=0)]
  transfers between devices with their start and end apart: 7 -> 7, of which waited for: 5 -> 5; matrix products, arithmetic and copies ran while one was open for 22% -> 23% of each run, Pallas kernels for 0% -> 0%
where the time goes in v1:
time: 618 us; the launch traced here: 609 us
  waiting for transfers between devices  271 us (44%)
  matrix products  138 us (22%)
  local copies, waits for them, and re-layouts  116 us (19%)
  other arithmetic  26.4 us (4%)
  starting transfers between devices  23.7 us (4%)
  blocking collectives  18.9 us (3%)
  between operations  14.6 us (2%)
    psum x2, waiting for transfers between devices, local(): image = lax.psum(partial_rows, 'by')  172 us
    all_to_all x2, waiting for transfers between devices, local(): lax.all_to_all(outgoing, 'wide', split_axis=0, concat_axis=0, tiled=True)  56.9 us
    dot_general x2, matrix products, local(): direct = jnp.einsum('tab,tbk->tak', tiles, col_panels, precision=highest)  52.9 us
    all_to_all x2, waiting for transfers between devices, local(): lax.all_to_all(placed, 'wide', split_axis=0, concat_axis=0, tiled=True)  41.6 us
    dot_general x2, matrix products, local(): mirror = jnp.einsum('tba,tbk->tak', tiles, row_panels, precision=highest)  40.7 us
    dot_general x4, local copies, waits for them, and re-layouts, local(): jnp.dot(slot_table, received, precision=highest)  22.9 us
    all_gather x2, blocking collectives, wrap_the_pages(): return lax.all_gather(original, axis_name=chip_axis).sum(axis=0)  18.9 us
    another operation x6, other arithmetic, local(): factor = jnp.linalg.cholesky(gram)  13 us
  transfers between devices with their start and end apart: 7, of which 5 were waited for; matrix products, arithmetic and copies ran while one was open for 23% of the time, Pallas kernels for 0%

profile of v1, /device:TPU:0, one launch (start us, length us, event | category | flops | bytes accessed | tf_op | source)
XLA Modules:
  0.0 608.6 jit_solution(606154744110531305)
XLA Ops:
  8.8 5.2 all-to-all-start
  22.6 21.3 %fusion.13 = f32[22,512,64]{1,2,0:T(8,128)} fusion(f32[22,512,512]{2,1,0:T(8,128)} %param.7, f32[22,512,64]{1,0,2:T(8,128)S(1)} %fusion.60), kind=kOutput, calls=%fused_computation.15 | convolution fusion | flops 4429185024 | bytes 28835840 | tf_op jit(solution)/shard_map/tba,tbk->tak/dot_general | solution.py:52
  43.9 5.3 copy.53
  49.2 6.3 %reshape.155 = f32[22,32768,1]{1,0,2:T(8,128)} reshape(f32[22,512,64]{2,1,0:T(8,128)} %copy.53) | data formatting | bytes 5767168 | tf_op jit(solution)/shard_map/reshape | solution.py:56
  63.2 4.5 all-to-all-start.2
  75.3 41.6 %all-to-all-done.2 = f32[8,3,32768]{2,1,0:T(4,128)} async-done(((f32[8,3,32768]{2,1,0:T(4,128)}), f32[8,3,32768]{2,1,0:T(4,128)}, u32[]{:S(2)}, u32[]{:S(2)}) %all-to-all-start.2) | async-done | bytes 3145760 | tf_op jit(solution)/shard_map/all_to_all | solution.py:58
  116.9 4.5 all-to-all-start.1
  125.3 45.2 %all-to-all-done.1 = f32[8,3,32768]{2,1,0:T(4,128)} async-done(((f32[8,3,32768]{2,1,0:T(4,128)}), f32[8,3,32768]{2,1,0:T(4,128)}, u32[]{:S(2)}, u32[]{:S(2)}) %all-to-all-start.1) | async-done | bytes 3145760 | tf_op jit(solution)/shard_map/all_to_all | solution.py:44
  170.5 5.5 all_to_all.30
  176.0 6.4 %dot_general.80 = f32[512,64,24]{1,0,2:T(8,128)} reshape(f32[32768,24]{0,1:T(8,128)} %bitcast.84) | data formatting | bytes 6291456 | tf_op jit(solution)/shard_map/dot_general | solution.py:45
  182.4 6.6 %copy.48 = f32[512,64,24]{0,2,1:T(8,128)} copy(f32[512,64,24]{1,0,2:T(8,128)} %dot_general.80) | data formatting | bytes 6291456 | tf_op jit(solution)/shard_map/dot_general | solution.py:45
  192.6 27.3 %fusion.10 = f32[22,512,64]{1,2,0:T(8,128)} fusion(f32[22,512,512]{2,1,0:T(8,128)} %param.7, f32[22,512,64]{1,0,2:T(8,128)S(1)} %fusion.37), kind=kOutput, calls=%fused_computation.14 | convolution fusion | flops 4429185024 | bytes 28835840 | tf_op jit(solution)/shard_map/tab,tbk->tak/dot_general | solution.py:51
  219.9 5.3 copy.50
  225.3 6.5 %reshape.143 = f32[22,32768]{1,0:T(8,128)} reshape(f32[22,512,64]{2,1,0:T(8,128)} %copy.50) | data formatting | bytes 5767168 | tf_op jit(solution)/shard_map/reshape | solution.py:54
  240.5 86.1 %all-reduce.3.cloned.1.call-done = f32[4096,64]{1,0:T(8,128)} async-done(((f32[4096,64]{1,0:T(8,128)}), f32[4096,64]{1,0:T(8,128)}) %all-reduce.3.cloned.1.call-update) | async-done | bytes 1048592 | tf_op jit(solution)/shard_map/psum | solution.py:61
  326.6 5.9 fusion.68
  332.5 9.4 %all-gather = f32[512,64]{1,0:T(8,128)S(1)} all-gather(f32[64,64]{1,0:T(8,128)S(1)} %fusion.68), channel_id=2, replica_groups=mesh['wide'=8,'by'=4] {'wide'}, dimensions={0}, use_global_device_ids=true | all-gather | bytes 147456 | tf_op jit(solution)/shard_map/all_gather | solution.py:10
  342.1 5.8 cholesky.44
  349.3 4.9 custom-call.6
  363.4 4.8 all-to-all-start.3
  372.0 19.4 %fusion.19 = f32[22,512,64]{1,2,0:T(8,128)S(1)} fusion(f32[22,512,512]{2,1,0:T(8,128)} %param.7, f32[22,512,64]{1,0,2:T(8,128)S(1)} %fusion.58), kind=kOutput, calls=%fused_computation.17 | convolution fusion | flops 4429185024 | bytes 28835840 | tf_op jit(solution)/shard_map/tba,tbk->tak/dot_general | solution.py:52
  395.4 4.6 reshape.157
  405.7 11.6 %all-to-all-done.3 = f32[8,3,32768]{2,1,0:T(4,128)} async-done(((f32[8,3,32768]{2,1,0:T(4,128)}), f32[8,3,32768]{2,1,0:T(4,128)}, u32[]{:S(2)}, u32[]{:S(2)}) %all-to-all-start.3) | async-done | bytes 3145760 | tf_op jit(solution)/shard_map/all_to_all | solution.py:44
  417.3 4.5 all-to-all-start.4
  425.7 4.9 dot_general.95
  430.6 5.0 copy.58
  437.3 25.6 %fusion.16 = f32[22,512,64]{1,2,0:T(8,128)S(1)} fusion(f32[22,512,512]{2,1,0:T(8,128)} %param.7, f32[22,512,64]{1,0,2:T(8,128)S(1)} %fusion.35), kind=kOutput, calls=%fused_computation.16 | convolution fusion | flops 4429185024 | bytes 28835840 | tf_op jit(solution)/shard_map/tab,tbk->tak/dot_general | solution.py:51
  484.0 86.0 %all-reduce.5.cloned.1.call-done = f32[4096,64]{1,0:T(8,128)} async-done(((f32[4096,64]{1,0:T(8,128)}), f32[4096,64]{1,0:T(8,128)}) %all-reduce.5.cloned.1.call-update) | async-done | bytes 1048592 | tf_op jit(solution)/shard_map/psum | solution.py:61
  570.0 5.9 fusion.69
  576.0 9.5 %all-gather.1 = f32[512,64]{1,0:T(8,128)S(1)} all-gather(f32[64,64]{1,0:T(8,128)S(1)} %fusion.69), channel_id=3, replica_groups=mesh['wide'=8,'by'=4] {'wide'}, dimensions={0}, use_global_device_ids=true | all-gather | bytes 147456 | tf_op jit(solution)/shard_map/all_gather | solution.py:10
  585.6 5.8 cholesky.55
  593.4 4.9 custom-call.7
  (71 shorter events, 97.7 us)
Async XLA Ops:
  8.8 54.4 %all-to-all-start = ((s32[8,1,3]{2,1,0:T(1,128)}), s32[8,1,3]{2,1,0:T(1,128)S(1)}, u32[]{:S(2)}, u32[]{:S(2)}) async-start(s32[8,1,3]{2,1,0:T(1,128)} %bitcast.1), calls=%async_computation | async-start | bytes 8192 | tf_op jit(solution)/shard_map/all_to_all | solution.py:32
  16.5 4.7 copy-start.2
  63.2 53.7 %all-to-all-start.2 = ((f32[8,3,32768]{2,1,0:T(4,128)}), f32[8,3,32768]{2,1,0:T(4,128)}, u32[]{:S(2)}, u32[]{:S(2)}) async-start(f32[8,3,32768]{2,1,0:T(4,128)} %copy.54), calls=%async_computation.2 | async-start | bytes 8388608 | tf_op jit(solution)/shard_map/all_to_all | solution.py:58
  116.9 53.7 %all-to-all-start.1 = ((f32[8,3,32768]{2,1,0:T(4,128)}), f32[8,3,32768]{2,1,0:T(4,128)}, u32[]{:S(2)}, u32[]{:S(2)}) async-start(f32[8,3,32768]{2,1,0:T(4,128)} %copy.47), calls=%async_computation.1 | async-start | bytes 8388608 | tf_op jit(solution)/shard_map/all_to_all | solution.py:44
  121.4 205.1 %all-reduce.3.cloned.1.call-start = ((), (), s32[]{:S(2)}) async-start(), calls=%async_computation.5 | async-start | bytes 4194304 | tf_op jit(solution)/shard_map/psum | solution.py:61
  326.6 27.6 %copy-start.1 = (f32[4096,64]{1,0:T(8,128)S(1)}, f32[4096,64]{1,0:T(8,128)}, u32[]{:S(2)}) copy-start(f32[4096,64]{1,0:T(8,128)} %all-reduce.3.cloned.1.call-done) | copy-start | bytes 3145732
  363.4 54.0 %all-to-all-start.3 = ((f32[8,3,32768]{2,1,0:T(4,128)}), f32[8,3,32768]{2,1,0:T(4,128)}, u32[]{:S(2)}, u32[]{:S(2)}) async-start(f32[8,3,32768]{2,1,0:T(4,128)} %copy.57), calls=%async_computation.3 | async-start | bytes 8388608 | tf_op jit(solution)/shard_map/all_to_all | solution.py:44
  417.3 56.1 %all-to-all-start.4 = ((f32[8,3,32768]{2,1,0:T(4,128)}), f32[8,3,32768]{2,1,0:T(4,128)}, u32[]{:S(2)}, u32[]{:S(2)}) async-start(f32[8,3,32768]{2,1,0:T(4,128)} %copy.64), calls=%async_computation.4 | async-start | bytes 8388608 | tf_op jit(solution)/shard_map/all_to_all | solution.py:58
  421.9 148.2 %all-reduce.5.cloned.1.call-start = ((), (), s32[]{:S(2)}) async-start(), calls=%async_computation.6 | async-start | bytes 4194304 | tf_op jit(solution)/shard_map/psum | solution.py:61
  570.0 28.2 %copy-start = (f32[4096,64]{1,0:T(8,128)S(1)}, f32[4096,64]{1,0:T(8,128)}, u32[]{:S(2)}) copy-start(f32[4096,64]{1,0:T(8,128)} %all-reduce.5.cloned.1.call-done) | copy-start | bytes 3145732
Sparse Core Ops, SparseCore 0:
  240.6 85.9 all-reduce.2
  484.2 85.8 all-reduce.4
